TPU v7x, 128 devices: a whole 4x4x4 slice. The times are simulated.
128 devices in a mesh: row: 16 (over x, z), col: 8 (over y, core).
Axes of the slice: x: 4, y: 4, z: 4, core: 2. Of those that a mesh axis runs over, the one named last changes fastest.
Arguments:
- amplitudes: bfloat16 [16384, 16384], P('row', 'col'), may hold values from -6 to 6
- integrals: bfloat16 [16384, 4096], P('col', 'row'), may hold values from -0.046875 to 0.046875
- amp_mask: int32 [128, 128], P('row', 'col'), may hold values 0 or 1
- int_mask: int32 [128, 32], P('col', 'row'), may hold values 0 or 1
Outputs:
- ladder: bfloat16 [16384, 4096], P('row', 'col')
All inputs are finite; a program needn't handle non-finite values. No bound on the sum of `amp_mask` or of `int_mask` on one device may be relied on, other than what follows from the above.
Results may differ from a plain program's by a relative error of at most 0.001.
Values may be sent and summed in bfloat16 or wider, within the bound.
A program may use at most 128 MiB of HBM per device.

v0:
```python
import jax
import jax.numpy as jnp
from jax import lax
from jax.sharding import PartitionSpec as P

TILE = 128


def expand(mask):
    spread = jnp.repeat(jnp.repeat(mask, TILE, axis=0), TILE, axis=1)
    return spread.astype(jnp.bfloat16)


def per_device(amplitudes, integrals, amp_mask, int_mask):
    sparse_amp = amplitudes * expand(amp_mask)
    sparse_int = integrals * expand(int_mask)
    partial_value = jnp.dot(
        sparse_amp,
        lax.all_gather(sparse_int, "row", axis=1, tiled=True),
        preferred_element_type=jnp.float32,
    )
    ladder = lax.psum_scatter(partial_value, "col", scatter_dimension=1, tiled=True)
    return ladder.astype(jnp.bfloat16)


def solution(mesh):
    in_specs = (P("row", "col"), P("col", "row"), P("row", "col"), P("col", "row"))
    out_specs = P("row", "col")
    return jax.shard_map(
        per_device, mesh=mesh, in_specs=in_specs, out_specs=out_specs, check_vma=False
    )
```

profile of v0, /device:TPU:1, one launch (start us, length us, event | category | flops | bytes accessed | tf_op | source)
XLA Modules:
  0.0 265.9 jit_solution(4168106295409174461)
XLA Ops:
  6.5 0.0 copy-start
  6.5 0.0 all-gather.2.cloned.1.call-start
  6.5 0.7 convert_element_type.28
  7.2 0.1 copy.5
  7.3 0.1 broadcast_in_dim.14
  7.4 5.8 %broadcast_in_dim.15 = bf16[2048,2,128]{2,1,0:T(2,128)(2,1)S(1)} broadcast(bf16[2048,2]{1,0:T(8,128)(2,1)S(1)} %bitcast.12), dimensions={0,1} | broadcast | bytes 1056768 | tf_op jit(solution)/shard_map/broadcast_in_dim | solution.py:10
  13.2 2.4 bitcast_multiply_fusion.2
  15.6 0.0 all-gather.2.cloned.1.call-update
  15.6 0.0 reduce-scatter.2.cloned.1.call-start
  15.6 0.0 copy-done
  15.7 121.9 %all-gather.2.cloned.1.call-done = bf16[2048,4096]{1,0:T(8,128)(2,1)} async-done(((bf16[2048,256]{1,0:T(8,128)(2,1)}), bf16[2048,4096]{1,0:T(8,128)(2,1)}) %all-gather.2.cloned.1.call-update) | async-done | bytes 16777232 | tf_op jit(solution)/shard_map/all_gather | solution.py:19
  137.5 0.0 copy-start.1
  137.6 4.5 %broadcast_in_dim.13 = bf16[1024,16,128]{2,1,0:T(8,128)(2,1)S(1)} broadcast(bf16[1024,16]{1,0:T(8,128)(2,1)S(1)} %bitcast.13), dimensions={0,1} | broadcast | bytes 4227072 | tf_op jit(solution)/shard_map/broadcast_in_dim | solution.py:10
  142.1 0.0 copy-done.1
  142.1 22.2 %fusion = f32[1024,4096]{1,0:T(8,128)} fusion(bf16[2048,4096]{1,0:T(8,128)(2,1)} %all-gather.2.cloned.1.call-done, bf16[1024,2048]{1,0:T(8,128)(2,1)S(1)} %copy-done.1, bf16[128,8,16,128]{3,2,1,0:T(8,128)(2,1)S(1)} %bitcast.11), kind=kOutput, calls=%fused_computation.1 | convolution fusion | flops 17181966336 | bytes 41943040 | tf_op jit(solution)/shard_map/dot_general | solution.py:17
  164.3 0.0 reduce-scatter.2.cloned.1.call-update
  164.3 92.0 %reduce-scatter.2.cloned.1.call-done = f32[1024,512]{1,0:T(8,128)} async-done(((f32[1024,4096]{1,0:T(8,128)}), f32[1024,512]{1,0:T(8,128)}) %reduce-scatter.2.cloned.1.call-update) | async-done | bytes 2097168 | tf_op jit(solution)/shard_map/reduce_scatter | solution.py:22
  256.3 2.7 %convert_element_type.31 = bf16[1024,512]{1,0:T(8,128)(2,1)} convert(f32[1024,512]{1,0:T(8,128)} %reduce-scatter.2.cloned.1.call-done) | non-fusion elementwise | flops 524288 | bytes 3145728 | tf_op jit(solution)/shard_map/convert_element_type | solution.py:23
  (2 shorter events, 0.0 us)
Async XLA Ops:
  6.5 9.1 %copy-start = (s32[8,16]{1,0:T(8,128)S(1)}, s32[8,16]{1,0:T(8,128)}, u32[]{:S(2)}) copy-start(s32[8,16]{1,0:T(8,128)} %param.6) | copy-start | bytes 1540
  6.5 131.0 %all-gather.2.cloned.1.call-start = ((), (), s32[]{:S(2)}) async-start(), calls=%async_computation.1 | async-start | bytes 17825792 | tf_op jit(solution)/shard_map/all_gather | solution.py:19
  15.6 240.8 %reduce-scatter.2.cloned.1.call-start = ((), (), s32[]{:S(2)}) async-start(), calls=%async_computation.2 | async-start | bytes 18874368 | tf_op jit(solution)/shard_map/reduce_scatter | solution.py:22
  137.5 4.5 %copy-start.1 = (bf16[1024,2048]{1,0:T(8,128)(2,1)S(1)}, bf16[1024,2048]{1,0:T(8,128)(2,1)}, u32[]{:S(2)}) copy-start(bf16[1024,2048]{1,0:T(8,128)(2,1)} %param.4) | copy-start | bytes 12582916
Sparse Core Ops, SparseCore 0:
  15.7 121.7 all-gather.1
  164.5 91.8 reduce-scatter.1
where the time goes:
time: 266 us
  waiting for transfers between devices  214 us (80%)
  matrix products  22.2 us (8%)
  between operations  13.4 us (5%)
  local copies, waits for them, and re-layouts  10.5 us (4%)
  other arithmetic  5.77 us (2%)
    all_gather x1, waiting for transfers between devices, per_device(): lax.all_gather(sparse_int, 'row', axis=1, tiled=True)  122 us
    reduce_scatter x1, waiting for transfers between devices, per_device(): lax.psum_scatter(partial_value, 'col', scatter_dimension=1, tiled=True)  92 us
    dot_general x1, matrix products, per_device(): jnp.dot(sparse_amp, lax.all_gather(sparse_int, 'row', axis=1, tiled=True)...  22.2 us
    broadcast_in_dim x4, local copies, waits for them, and re-layouts, expand(): spread = jnp.repeat(jnp.repeat(mask, TILE, axis=0), TILE, axis=1)  10.4 us
  transfers between devices with their start and end apart: 2, of which 2 were waited for; matrix products, arithmetic and copies ran while one was open for 0% of the time, Pallas kernels for 0%

commit v1 on v0

--- a/solution.py
+++ b/solution.py
@@ -14,10 +14,16 @@
 def per_device(amplitudes, integrals, amp_mask, int_mask):
     sparse_amp = amplitudes * expand(amp_mask)
     sparse_int = integrals * expand(int_mask)
+
+    def search_the_forms(frame, peer_axis, pos_dim):
+        front = lax.psum(1, peer_axis)
+        outer = jnp.stack(front * [frame])
+        reached = lax.all_to_all(outer, peer_axis, 0, 0)
+        y1 = jnp.concatenate(reached, pos_dim)
+        return y1
+
     partial_value = jnp.dot(
-        sparse_amp,
-        lax.all_gather(sparse_int, "row", axis=1, tiled=True),
-        preferred_element_type=jnp.float32,
+        sparse_amp, search_the_forms(sparse_int, "row", 1), preferred_element_type=jnp.float32
     )
     ladder = lax.psum_scatter(partial_value, "col", scatter_dimension=1, tiled=True)
     return ladder.astype(jnp.bfloat16)

time: 266 us -> 457 us (1.72)
  waiting for transfers between devices: 214 us -> 391 us
  starting transfers between devices: 0.04 us -> 8.64 us
  local copies, waits for them, and re-layouts: 10.5 us -> 17.1 us
    all_to_all x0 -> x1, waiting for transfers between devices: none -> 293 us  [search_the_forms(): reached = lax.all_to_all(outer, peer_axis, 0, 0)]
    all_gather x1 -> x0, waiting for transfers between devices: 122 us -> none  [per_device(): lax.all_gather(sparse_int, 'row', axis=1, tiled=True)]
    all_to_all x0 -> x1, starting transfers between devices: none -> 8.6 us  [search_the_forms(): reached = lax.all_to_all(outer, peer_axis, 0, 0)]
    another operation x0 -> x1, local copies, waits for them, and re-layouts: none -> 5.97 us  [search_the_forms(): outer = jnp.stack(front * [frame])]
    reduce_scatter x1, waiting for transfers between devices: 92 us -> 97.3 us  [per_device(): lax.psum_scatter(partial_value, 'col', scatter_dimension=1, tiled=True)]
where the time goes in v1:
time: 457 us
  waiting for transfers between devices  391 us (86%)
  matrix products  22.4 us (5%)
  local copies, waits for them, and re-layouts  17.1 us (4%)
  between operations  13.5 us (3%)
  starting transfers between devices  8.64 us (2%)
  other arithmetic  4.79 us (1%)
    all_to_all x1, waiting for transfers between devices, search_the_forms(): reached = lax.all_to_all(outer, peer_axis, 0, 0)  293 us
    reduce_scatter x1, waiting for transfers between devices, per_device(): lax.psum_scatter(partial_value, 'col', scatter_dimension=1, tiled=True)  97.3 us
    dot_general x1, matrix products, per_device(): jnp.dot(sparse_amp, search_the_forms(sparse_int, 'row', 1), preferred_ele...  22.4 us
    broadcast_in_dim x4, local copies, waits for them, and re-layouts, expand(): spread = jnp.repeat(jnp.repeat(mask, TILE, axis=0), TILE, axis=1)  10.4 us
  transfers between devices with their start and end apart: 2, of which 2 were waited for; matrix products, arithmetic and copies ran while one was open for 0% of the time, Pallas kernels for 0%

profile of v1, /device:TPU:1, one launch (start us, length us, event | category | flops | bytes accessed | tf_op | source)
XLA Modules:
  0.0 457.0 jit_solution(6361364830935335135)
XLA Ops:
  6.5 0.7 convert_element_type.28
  7.2 0.1 copy.6
  7.3 0.1 broadcast_in_dim.14
  7.4 5.8 %broadcast_in_dim.15 = bf16[2048,2,128]{2,1,0:T(2,128)(2,1)S(1)} broadcast(bf16[2048,2]{1,0:T(8,128)(2,1)S(1)} %bitcast.15), dimensions={0,1} | broadcast | bytes 1056768 | tf_op jit(solution)/shard_map/broadcast_in_dim | solution.py:10
  13.2 1.4 bitcast_multiply_fusion.2
  14.6 0.6 copy.7
  15.2 6.0 %stack.2 = bf16[16,2048,256]{1,2,0:T(8,128)(2,1)} broadcast(bf16[2048,256]{0,1:T(8,128)(2,1)S(1)} %copy.7), dimensions={1,2} | broadcast | bytes 17825792 | tf_op jit(solution)/shard_map/stack | solution.py:20
  21.2 0.0 copy-start
  21.2 8.6 %all-to-all-start = ((bf16[16,2048,256]{1,2,0:T(8,128)(2,1)}), bf16[16,2048,256]{1,2,0:T(8,128)(2,1)}, u32[]{:S(2)}, u32[]{:S(2)}) async-start(bf16[16,2048,256]{1,2,0:T(8,128)(2,1)} %stack.2), calls=%async_computation | async-start | bytes 33554432 | tf_op jit(solution)/shard_map/all_to_all | solution.py:21
  29.8 0.0 reduce-scatter.2.cloned.1.call-start
  29.9 0.0 copy-done
  29.9 293.2 %all-to-all-done = bf16[16,2048,256]{1,2,0:T(8,128)(2,1)} async-done(((bf16[16,2048,256]{1,2,0:T(8,128)(2,1)}), bf16[16,2048,256]{1,2,0:T(8,128)(2,1)}, u32[]{:S(2)}, u32[]{:S(2)}) %all-to-all-start) | async-done | bytes 16777248 | tf_op jit(solution)/shard_map/all_to_all | solution.py:21
  323.1 0.0 copy-start.1
  323.2 4.5 broadcast_in_dim.13
  327.6 0.0 copy-done.1
  327.7 22.4 %fusion = f32[1024,4096]{1,0:T(8,128)} fusion(bf16[2048,4096]{0,1:T(8,128)(2,1)} %bitcast.3, bf16[1024,2048]{1,0:T(8,128)(2,1)S(1)} %copy-done.1, bf16[128,8,16,128]{3,2,1,0:T(8,128)(2,1)S(1)} %bitcast.14), kind=kOutput, calls=%fused_computation.1 | convolution fusion | flops 17181966336 | bytes 41943040 | tf_op jit(solution)/shard_map/dot_general | solution.py:25
  350.1 0.0 reduce-scatter.2.cloned.1.call-update
  350.1 97.3 %reduce-scatter.2.cloned.1.call-done = f32[1024,512]{1,0:T(8,128)} async-done(((f32[1024,4096]{1,0:T(8,128)}), f32[1024,512]{1,0:T(8,128)}) %reduce-scatter.2.cloned.1.call-update) | async-done | bytes 2097168 | tf_op jit(solution)/shard_map/reduce_scatter | solution.py:28
  447.4 2.7 convert_element_type.31
  (2 shorter events, 0.0 us)
Async XLA Ops:
  21.2 8.7 %copy-start = (s32[8,16]{1,0:T(8,128)S(1)}, s32[8,16]{1,0:T(8,128)}, u32[]{:S(2)}) copy-start(s32[8,16]{1,0:T(8,128)} %param.6) | copy-start | bytes 1540
  21.2 301.9 %all-to-all-start = ((bf16[16,2048,256]{1,2,0:T(8,128)(2,1)}), bf16[16,2048,256]{1,2,0:T(8,128)(2,1)}, u32[]{:S(2)}, u32[]{:S(2)}) async-start(bf16[16,2048,256]{1,2,0:T(8,128)(2,1)} %stack.2), calls=%async_computation | async-start | bytes 33554432 | tf_op jit(solution)/shard_map/all_to_all | solution.py:21
  29.8 417.6 %reduce-scatter.2.cloned.1.call-start = ((), (), s32[]{:S(2)}) async-start(), calls=%async_computation.2 | async-start | bytes 18874368 | tf_op jit(solution)/shard_map/reduce_scatter | solution.py:28
  323.1 4.5 copy-start.1
Sparse Core Ops, SparseCore 0:
  350.2 97.1 reduce-scatter.1
